TPU v7x, 256 devices: a whole 4x4x8 slice. The times are simulated.
256 devices in a mesh: row: 32 (over z_lo, y, x), col: 8 (over z_hi, core).
Axes of the slice: x: 4, y: 4, z: 8 (z_hi: 4, z_lo: 2; z = z_hi * 2 + z_lo), core: 2. Of those that a mesh axis runs over, the one named last changes fastest.
Arguments:
- positions: float32 [3, 14336], P(None, ('row', 'col')), as said below
- polarizability: float32 [14336], P(('row', 'col')), may hold values from 0.04 to 0.16
- seeds: float32 [3, 16, 14336], P(None, None, ('row', 'col')), may hold values from -6 to 6
- dipoles: float32 [3, 16, 14336], P(None, None, ('row', 'col')), may hold values from -1.8 to 1.8
- tile_mask: int32 [256, 256], P('row', 'col'), may hold values from 0 to 1, as said below
Outputs:
- adjoint_field: float32 [3, 16, 14336], P(None, None, ('row', 'col'))
- gradient: float32 [3, 14336], P(None, ('row', 'col'))
Inputs may be any that keep to these rules, and one draw needn't show every extreme that they name: `positions`: beads lie near distinct points of a unit cubic lattice, each coordinate within 0.3 of its point; the points fill a roughly spherical droplet, and the beads of one block are spatially compact clusters of neighbouring points. Read as m_ab = tile_mask[a, (b % 8) * 32 + b // 8], m_ab is 1 exactly when the axis-aligned boxes spanned by the lattice points of blocks a and b lie within a distance of 6 of each other; so the table is symmetric with ones on the diagonal.
All inputs are finite; a program needn't handle non-finite values.
Results may differ from a plain program's by a relative error of at most 0.0003.
Values sent between devices are 32-bit elements; how exact they have to be, the bound alone decides.
No kernel may reach another device: no remote copies, remote signals or barrier semaphores. Data moves between devices by JAX's collectives and lax.ppermute only.
A program may use at most 64 MiB of HBM per device.

v0:
```python
import jax
import jax.numpy as jnp
from jax import lax
from jax.sharding import PartitionSpec as P

THOLE_DAMPING = 0.39
HIGHEST = lax.Precision.HIGHEST


def cut_along(x, dim, devices):
    before, after = (x.shape[:dim], x.shape[dim + 1 :])
    return jnp.moveaxis(x.reshape(*before, devices, -1, *after), dim, 0)


def sent_and_summed(x, axis, dim):
    pieces = cut_along(x, dim, lax.axis_size(axis))
    arrived = lax.all_to_all(pieces, axis, split_axis=0, concat_axis=0, tiled=True)
    return arrived.sum(axis=0)


def rows_first(arrays, axis, dims):
    turned = [jnp.moveaxis(a, dim, 0) for a, dim in zip(arrays, dims)]
    widths = [t[0].size for t in turned]
    both = jnp.concatenate([t.reshape(-1, w) for t, w in zip(turned, widths)], axis=1)
    out = lax.all_gather(both, axis, axis=0, tiled=True)
    pieces = jnp.split(out, [sum(widths[:k]) for k in range(1, len(widths))], axis=1)
    return tuple(
        (
            jnp.moveaxis(b.reshape(-1, *t.shape[1:]), 0, dim)
            for b, t, dim in zip(pieces, turned, dims)
        )
    )


def from_everyone(x, axis):
    devices = lax.axis_size(axis)
    return lax.all_to_all(jnp.broadcast_to(x[None], (devices, *x.shape)), axis, 0, 0, tiled=True)


def laid_out(pieces, dim):
    dims = list(pieces.shape[1:])
    dims[dim] *= pieces.shape[0]
    return jnp.moveaxis(pieces, 0, dim).reshape(dims)


def gathered_copies(x, axis, dim):
    pieces = from_everyone(x, axis)
    return laid_out(pieces, dim)


def pair_terms(row_geom, col_geom, keep_mask):
    offset = row_geom[:3, :, None] - col_geom[:3, None, :]
    dist_sq = jnp.sum(offset * offset, axis=0)
    dist_sq = jnp.where(keep_mask > 0.0, dist_sq, 1.0)
    inverse = lax.rsqrt(dist_sq)
    damping = (
        THOLE_DAMPING * dist_sq * (dist_sq * inverse) * row_geom[3][:, None] * col_geom[3][None, :]
    )
    damp_exp = jnp.exp(-damping)
    inv_cube = keep_mask * inverse * inverse * inverse
    isotropic = (1.0 - damp_exp) * inv_cube
    radial = 3.0 * (1.0 - (1.0 + damping) * damp_exp) * inv_cube * inverse * inverse
    tensor = radial[None, None] * offset[:, None] * offset[None, :]
    return (tensor, isotropic)


def apply_rows(tensor, isotropic, vector):
    result = jnp.einsum("abij,bpj->api", tensor, vector, precision=HIGHEST)
    return result - jnp.einsum("ij,apj->api", isotropic, vector, precision=HIGHEST)


def apply_cols(tensor, isotropic, vector):
    result = jnp.einsum("abij,bpi->apj", tensor, vector, precision=HIGHEST)
    return result - jnp.einsum("ij,api->apj", isotropic, vector, precision=HIGHEST)


def split_rows(values, groups):
    shaped = values.reshape(values.shape[:-1] + (groups, values.shape[-1] // groups))
    return jnp.moveaxis(shaped, -2, 0)


def join_rows(values):
    shifted = jnp.moveaxis(values, 0, -2)
    return shifted.reshape(shifted.shape[:-2] + (-1,))


def local(positions, polarizability, seeds, dipoles, tile_mask):
    bead_count = positions.shape[1]
    probes = seeds.shape[1]
    row_count = lax.axis_size("row")
    col_count = lax.axis_size("col")
    row_at = lax.axis_index("row")
    col_at = lax.axis_index("col")
    span_cols = bead_count * row_count
    geometry = jnp.concatenate([positions, lax.rsqrt(polarizability)[None, :]], axis=0)
    start_vector = polarizability[None, None, :] * seeds
    col_slot = jnp.arange(span_cols, dtype=jnp.int32)
    col_group = col_slot // bead_count
    col_global = (col_group * col_count + col_at) * bead_count + col_slot % bead_count
    row_global = (row_at * col_count + jnp.arange(col_count, dtype=jnp.int32))[:, None] * bead_count
    row_global = row_global + jnp.arange(bead_count, dtype=jnp.int32)[None, :]
    selector = (col_group[None, :] == jnp.arange(row_count, dtype=jnp.int32)[:, None]).astype(
        jnp.float32
    )
    col_mask = jnp.dot(tile_mask.astype(jnp.float32), selector, precision=HIGHEST)
    keep_mask = col_mask[:, None, :] * (row_global[:, :, None] != col_global[None, None, :]).astype(
        jnp.float32
    )

    def sweep_cols(vector_rows_split, rows_split, geom_cols):

        def one_shard(running, inputs):
            geom_rows, keep_rows, vector_rows = inputs
            tensor, isotropic = pair_terms(geom_rows, geom_cols, keep_rows)
            return (running + apply_cols(tensor, isotropic, vector_rows), None)

        empty_sum = jnp.zeros((3, probes, span_cols), jnp.float32)
        partial_cols, ignored = lax.scan(
            one_shard, empty_sum, (rows_split, keep_mask, vector_rows_split)
        )
        return sent_and_summed(partial_cols, "row", 2)

    geom_rows_all, start_rows = rows_first((geometry, start_vector), "col", (1, 2))
    geom_cols, dipole_cols = rows_first((geometry, dipoles), "row", (1, 2))
    rows_split = split_rows(geom_rows_all, col_count)
    field_one = seeds + sweep_cols(split_rows(start_rows, col_count), rows_split, geom_cols)
    next_vector = polarizability[None, None, :] * field_one
    next_rows = gathered_copies(next_vector, "col", 2)
    field_two = seeds + sweep_cols(split_rows(next_rows, col_count), rows_split, geom_cols)
    adjoint = polarizability[None, None, :] * field_two
    adjoint_rows = gathered_copies(adjoint, "col", 2)

    def pair_score(geom_rows, geom_all, keep_rows, adjoint_one):
        tensor, isotropic = pair_terms(geom_rows, geom_all, keep_rows)
        return jnp.sum(adjoint_one * apply_rows(tensor, isotropic, dipole_cols))

    slopes = jax.grad(pair_score, argnums=(0, 1))

    def force_shard(running, inputs):
        geom_rows, keep_rows, adjoint_one = inputs
        slope_rows, slope_cols = slopes(geom_rows, geom_cols, keep_rows, adjoint_one)
        return (running + slope_cols[:3], slope_rows[:3])

    empty_force = jnp.zeros((3, span_cols), jnp.float32)
    force_cols, force_split = lax.scan(
        force_shard, empty_force, (rows_split, keep_mask, split_rows(adjoint_rows, col_count))
    )
    force_rows = join_rows(force_split)
    gradient = sent_and_summed(force_rows, "col", 1) + sent_and_summed(force_cols, "row", 1)
    return (field_two, gradient)


def solution(mesh):
    in_specs = (
        P(None, ("row", "col")),
        P(("row", "col")),
        P(None, None, ("row", "col")),
        P(None, None, ("row", "col")),
        P("row", "col"),
    )
    out_specs = (P(None, None, ("row", "col")), P(None, ("row", "col")))
    return jax.shard_map(local, mesh=mesh, in_specs=in_specs, out_specs=out_specs, check_vma=False)
```

profile of v0, /device:TPU:1, one launch (start us, length us, event | category | flops | bytes accessed | tf_op | source)
XLA Modules:
  0.0 371.4 jit_solution(5194163001965535177)
XLA Ops:
  3.7 73.9 %all_gather.7 = f32[1792,52]{1,0:T(8,128)S(1)} all-gather(f32[56,52]{1,0:T(8,128)S(1)} %copy.28), channel_id=1, replica_groups=mesh['row'=32,'col'=8] {'row'}, dimensions={0}, use_global_device_ids=true | all-gather | bytes 384384 | tf_op jit(solution)/shard_map/all_gather | solution.py:25
  78.1 31.7 %all_gather.6 = f32[448,52]{1,0:T(8,128)S(1)} all-gather(f32[56,52]{1,0:T(8,128)S(1)} %copy.25), channel_id=1, replica_groups=mesh['row'=32,'col'=8] {'col'}, dimensions={0}, use_global_device_ids=true | all-gather | bytes 104832 | tf_op jit(solution)/shard_map/all_gather | solution.py:25
  110.4 2.0 compare_select_fusion
  112.4 44.9 %while.35 = (s32[]{:T(128)}, f32[3,16,1792]{2,1,0:T(8,128)S(1)}, f32[8,3,16,56]{3,0,2,1:T(8,128)S(1)}, f32[8,56,1792]{2,1,0:T(8,128)}, f32[8,4,56]{2,1,0:T(4,128...) while((s32[]{:T(128)}, f32[3,16,1792]{2,1,0:T(8,128)S(1)}, ...), condition=%wide.region_2.3_spmd.clone, body=%wide.region_0.2_spmd.clone.sunk | while | flops 236888064 | bytes 9123691 | solution.py:118
  114.2 2.1 fusion.132
  116.3 1.7 fusion.133
  119.9 2.1 fusion.132
  121.9 1.7 fusion.133
  125.5 2.1 fusion.132
  127.5 1.7 fusion.133
  131.1 2.1 fusion.132
  133.2 1.7 fusion.133
  136.7 2.1 fusion.132
  138.8 1.7 fusion.133
  142.3 2.1 fusion.132
  144.4 1.7 fusion.133
  147.9 2.1 fusion.132
  153.6 2.1 fusion.132
  159.5 12.1 %all_to_all.30 = f32[32,1,2688]{2,1,0:T(1,128)S(1)} all-to-all(f32[32,1,2688]{2,1,0:T(1,128)S(1)} %reshape.386), channel_id=1, replica_groups=mesh['row'=32,'col'=8] {'row'}, dimensions={0} | all-to-all | bytes 688128 | tf_op jit(solution)/shard_map/all_to_all | solution.py:17
  175.1 6.4 %all-to-all-start.1 = ((f32[8,1,2688]{2,1,0:T(1,128)}), f32[8,1,2688]{2,1,0:T(1,128)S(1)}, u32[]{:S(2)}, u32[]{:S(2)}) async-start(f32[8,1,2688]{2,1,0:T(1,128)} %reshape.388), calls=%async_computation.1 | async-start | bytes 172032 | tf_op jit(solution)/shard_map/all_to_all | solution.py:37
  181.6 7.6 %all-to-all-done.1 = f32[8,1,2688]{2,1,0:T(1,128)S(1)} async-done(((f32[8,1,2688]{2,1,0:T(1,128)}), f32[8,1,2688]{2,1,0:T(1,128)S(1)}, u32[]{:S(2)}, u32[]{:S(2)}) %all-to-all-start.1) | async-done | bytes 86048 | tf_op jit(solution)/shard_map/all_to_all | solution.py:37
  190.1 44.6 %while.36 = (s32[]{:T(128)}, f32[3,16,1792]{2,1,0:T(8,128)S(1)}, f32[8,3,16,56]{3,2,1,0:T(8,128)S(1)}, f32[8,56,1792]{2,1,0:T(8,128)}, f32[8,4,56]{2,1,0:T(4,128...) while((s32[]{:T(128)}, f32[3,16,1792]{2,1,0:T(8,128)S(1)}, ...), condition=%wide.region_6.7_spmd.clone, body=%wide.region_4.6_spmd.clone.sunk | while | flops 236888064 | bytes 9131659 | solution.py:118
  191.9 2.0 fusion.138
  197.5 2.0 fusion.138
  199.6 1.7 fusion.139
  203.1 2.0 fusion.138
  208.7 2.0 fusion.138
  210.7 1.7 fusion.139
  214.2 2.0 fusion.138
  219.8 2.0 fusion.138
  225.4 2.0 fusion.138
  230.9 2.0 fusion.138
  236.8 12.2 %all_to_all.31 = f32[32,1,2688]{2,1,0:T(1,128)S(1)} all-to-all(f32[32,1,2688]{2,1,0:T(1,128)S(1)} %reshape.390), channel_id=1, replica_groups=mesh['row'=32,'col'=8] {'row'}, dimensions={0} | all-to-all | bytes 688128 | tf_op jit(solution)/shard_map/all_to_all | solution.py:17
  252.6 5.5 %all-to-all-start.3 = ((f32[8,1,2688]{2,1,0:T(1,128)}), f32[8,1,2688]{2,1,0:T(1,128)S(1)}, u32[]{:S(2)}, u32[]{:S(2)}) async-start(f32[8,1,2688]{2,1,0:T(1,128)} %reshape.392), calls=%async_computation.3 | async-start | bytes 172032 | tf_op jit(solution)/shard_map/all_to_all | solution.py:37
  258.7 7.0 %all-to-all-done.3 = f32[8,1,2688]{2,1,0:T(1,128)S(1)} async-done(((f32[8,1,2688]{2,1,0:T(1,128)}), f32[8,1,2688]{2,1,0:T(1,128)S(1)}, u32[]{:S(2)}, u32[]{:S(2)}) %all-to-all-start.3) | async-done | bytes 86048 | tf_op jit(solution)/shard_map/all_to_all | solution.py:37
  266.8 80.1 %while.37 = (s32[]{:T(128)}, f32[3,1792]{1,0:T(4,128)S(1)}, f32[8,3,56]{2,1,0:T(4,128)S(1)}, f32[8,56,1792]{2,1,0:T(8,128)}, f32[8,4,56]{2,1,0:T(4,128)S(1)}, /*...) while((s32[]{:T(128)}, f32[3,1792]{1,0:T(4,128)S(1)}, ...), condition=%wide.region_17.18_spmd.clone, body=%wide.region_8.17_spmd.clone.sunk | while | flops 248187520 | bytes 19899200 | solution.py:145
  268.6 3.7 fusion.142
  272.4 2.0 multiply_reduce_fusion.9
  274.4 1.7 fusion.144
  278.6 3.7 fusion.142
  282.4 2.0 multiply_reduce_fusion.9
  284.4 1.7 fusion.144
  288.6 3.7 fusion.142
  292.4 2.0 multiply_reduce_fusion.9
  294.4 1.7 fusion.144
  298.6 3.7 fusion.142
  302.5 2.0 multiply_reduce_fusion.9
  304.4 1.7 fusion.144
  308.6 3.7 fusion.142
  312.5 2.0 multiply_reduce_fusion.9
  314.4 1.7 fusion.144
  318.6 3.7 fusion.142
  322.5 2.0 multiply_reduce_fusion.9
  324.4 1.7 fusion.144
  328.6 3.7 fusion.142
  332.5 2.0 multiply_reduce_fusion.9
  334.4 1.7 fusion.144
  338.6 3.7 fusion.142
  342.5 2.0 multiply_reduce_fusion.9
  344.4 1.7 fusion.144
  347.5 4.3 %all-to-all-start.4 = ((f32[8,1,168]{2,1,0:T(1,128)}), f32[8,1,168]{2,1,0:T(1,128)S(1)}, u32[]{:S(2)}, u32[]{:S(2)}) async-start(f32[8,1,168]{2,1,0:T(1,128)} %reshape.394), calls=%async_computation.4 | async-start | bytes 16384 | tf_op jit(solution)/shard_map/all_to_all | solution.py:17
  352.7 6.2 %all-to-all-done.4 = f32[8,1,168]{2,1,0:T(1,128)S(1)} async-done(((f32[8,1,168]{2,1,0:T(1,128)}), f32[8,1,168]{2,1,0:T(1,128)S(1)}, u32[]{:S(2)}, u32[]{:S(2)}) %all-to-all-start.4) | async-done | bytes 5408 | tf_op jit(solution)/shard_map/all_to_all | solution.py:17
  358.9 3.9 %all-to-all-start.5 = ((f32[32,1,168]{2,1,0:T(1,128)}), f32[32,1,168]{2,1,0:T(1,128)S(1)}, u32[]{:S(2)}, u32[]{:S(2)}) async-start(f32[32,1,168]{2,1,0:T(1,128)} %reshape.396), calls=%async_computation.5 | async-start | bytes 65536 | tf_op jit(solution)/shard_map/all_to_all | solution.py:17
  363.5 6.4 %all-to-all-done.5 = f32[32,1,168]{2,1,0:T(1,128)S(1)} async-done(((f32[32,1,168]{2,1,0:T(1,128)}), f32[32,1,168]{2,1,0:T(1,128)S(1)}, u32[]{:S(2)}, u32[]{:S(2)}) %all-to-all-start.5) | async-done | bytes 21536 | tf_op jit(solution)/shard_map/all_to_all | solution.py:17
  (303 shorter events, 83.9 us)
Async XLA Ops:
  77.7 32.6 %copy-start.2 = (s32[8,32]{1,0:T(8,128)S(1)}, s32[8,32]{1,0:T(8,128)}, u32[]{:S(2)}) copy-start(s32[8,32]{1,0:T(8,128)} %param.15) | copy-start | bytes 3076
  172.1 2.1 copy-start
  172.1 2.2 copy-start.1
  175.1 14.0 %all-to-all-start.1 = ((f32[8,1,2688]{2,1,0:T(1,128)}), f32[8,1,2688]{2,1,0:T(1,128)S(1)}, u32[]{:S(2)}, u32[]{:S(2)}) async-start(f32[8,1,2688]{2,1,0:T(1,128)} %reshape.388), calls=%async_computation.1 | async-start | bytes 172032 | tf_op jit(solution)/shard_map/all_to_all | solution.py:37
  252.6 13.1 %all-to-all-start.3 = ((f32[8,1,2688]{2,1,0:T(1,128)}), f32[8,1,2688]{2,1,0:T(1,128)S(1)}, u32[]{:S(2)}, u32[]{:S(2)}) async-start(f32[8,1,2688]{2,1,0:T(1,128)} %reshape.392), calls=%async_computation.3 | async-start | bytes 172032 | tf_op jit(solution)/shard_map/all_to_all | solution.py:37
  347.5 11.3 %all-to-all-start.4 = ((f32[8,1,168]{2,1,0:T(1,128)}), f32[8,1,168]{2,1,0:T(1,128)S(1)}, u32[]{:S(2)}, u32[]{:S(2)}) async-start(f32[8,1,168]{2,1,0:T(1,128)} %reshape.394), calls=%async_computation.4 | async-start | bytes 16384 | tf_op jit(solution)/shard_map/all_to_all | solution.py:17
  358.9 11.1 %all-to-all-start.5 = ((f32[32,1,168]{2,1,0:T(1,128)}), f32[32,1,168]{2,1,0:T(1,128)S(1)}, u32[]{:S(2)}, u32[]{:S(2)}) async-start(f32[32,1,168]{2,1,0:T(1,128)} %reshape.396), calls=%async_computation.5 | async-start | bytes 65536 | tf_op jit(solution)/shard_map/all_to_all | solution.py:17
where the time goes:
time: 374 us; the launch traced here: 371 us
  blocking collectives  130 us (35%)
  matrix products  105 us (28%)
  other arithmetic  72.7 us (19%)
  waiting for transfers between devices  27.2 us (7%)
  starting transfers between devices  20.1 us (5%)
  local copies, waits for them, and re-layouts  13.2 us (4%)
    all_gather x2, blocking collectives, rows_first(): out = lax.all_gather(both, axis, axis=0, tiled=True)  106 us
    dot_general x16, matrix products, apply_cols(): result = jnp.einsum('abij,bpi->apj', tensor, vector, precision=HIGHEST)  32.8 us
    mul x24, other arithmetic, pair_terms(): 3.0 * (1.0 - (1.0 + damping) * damp_exp) * inv_cube * inverse * inverse  31 us
    dot_general x8, matrix products, apply_rows(): result = jnp.einsum('abij,bpj->api', tensor, vector, precision=HIGHEST)  29.3 us
    dot_general x16, matrix products, apply_cols(): jnp.einsum('ij,api->apj', isotropic, vector, precision=HIGHEST)  27.4 us
    all_to_all x2, blocking collectives, sent_and_summed(): lax.all_to_all(pieces, axis, split_axis=0, concat_axis=0, tiled=True)  24.3 us
    dot_general x8, matrix products, apply_rows(): jnp.einsum('ij,apj->api', isotropic, vector, precision=HIGHEST)  15.7 us
    all_to_all x2, waiting for transfers between devices, from_everyone(): lax.all_to_all(jnp.broadcast_to(x[None], (devices, *x.shape)), axis, 0, 0...  14.6 us
  transfers between devices with their start and end apart: 4, of which 4 were waited for; matrix products, arithmetic and copies ran while one was open for 1% of the time, Pallas kernels for 0%

commit v1 on v0

--- a/solution.py
+++ b/solution.py
@@ -22,7 +22,10 @@
     turned = [jnp.moveaxis(a, dim, 0) for a, dim in zip(arrays, dims)]
     widths = [t[0].size for t in turned]
     both = jnp.concatenate([t.reshape(-1, w) for t, w in zip(turned, widths)], axis=1)
-    out = lax.all_gather(both, axis, axis=0, tiled=True)
+    count = lax.axis_size(axis)
+    shards = jnp.stack([both for _ in range(count)])
+    shards = lax.all_to_all(shards, axis, split_axis=0, concat_axis=0)
+    out = jnp.concatenate(shards, axis=0)
     pieces = jnp.split(out, [sum(widths[:k]) for k in range(1, len(widths))], axis=1)
     return tuple(
         (

time: 374 us -> 304 us (0.81)
  blocking collectives: 130 us -> 24.4 us
  starting transfers between devices: 20.1 us -> 38 us
  waiting for transfers between devices: 27.2 us -> 37.8 us
    all_gather x2 -> x0, blocking collectives: 106 us -> none  [rows_first(): out = lax.all_gather(both, axis, axis=0, tiled=True)]
    all_to_all x0 -> x2, starting transfers between devices: none -> 17.4 us  [rows_first(): shards = lax.all_to_all(shards, axis, split_axis=0, concat_axis=0)]
    all_to_all x0 -> x2, waiting for transfers between devices: none -> 10 us  [rows_first(): shards = lax.all_to_all(shards, axis, split_axis=0, concat_axis=0)]
    unnamed x22 -> x25, local copies, waits for them, and re-layouts: 7.47 us -> 9.89 us
  transfers between devices with their start and end apart: 4 -> 6, of which waited for: 4 -> 6; matrix products, arithmetic and copies ran while one was open for 1% -> 3% of each run, Pallas kernels for 0% -> 0%
where the time goes in v1:
time: 304 us; the launch traced here: 300 us
  matrix products  106 us (35%)
  other arithmetic  75.2 us (25%)
  starting transfers between devices  38 us (12%)
  waiting for transfers between devices  37.8 us (12%)
  blocking collectives  24.4 us (8%)
  local copies, waits for them, and re-layouts  15.9 us (5%)
    dot_general x16, matrix products, apply_cols(): result = jnp.einsum('abij,bpi->apj', tensor, vector, precision=HIGHEST)  33 us
    mul x24, other arithmetic, pair_terms(): 3.0 * (1.0 - (1.0 + damping) * damp_exp) * inv_cube * inverse * inverse  30.9 us
    dot_general x8, matrix products, apply_rows(): result = jnp.einsum('abij,bpj->api', tensor, vector, precision=HIGHEST)  29.9 us
    dot_general x16, matrix products, apply_cols(): jnp.einsum('ij,api->apj', isotropic, vector, precision=HIGHEST)  27.5 us
    all_to_all x2, blocking collectives, sent_and_summed(): lax.all_to_all(pieces, axis, split_axis=0, concat_axis=0, tiled=True)  24.4 us
    all_to_all x2, starting transfers between devices, rows_first(): shards = lax.all_to_all(shards, axis, split_axis=0, concat_axis=0)  17.4 us
    dot_general x8, matrix products, apply_rows(): jnp.einsum('ij,apj->api', isotropic, vector, precision=HIGHEST)  15.7 us
    all_to_all x2, waiting for transfers between devices, from_everyone(): lax.all_to_all(jnp.broadcast_to(x[None], (devices, *x.shape)), axis, 0, 0...  15.1 us
  transfers between devices with their start and end apart: 6, of which 6 were waited for; matrix products, arithmetic and copies ran while one was open for 3% of the time, Pallas kernels for 0%

profile of v1, /device:TPU:1, one launch (start us, length us, event | category | flops | bytes accessed | tf_op | source)
XLA Modules:
  0.0 300.5 jit_solution(1577313185306925809)
XLA Ops:
  4.4 10.0 %all-to-all-start = ((f32[8,1,2912]{2,1,0:T(1,128)}), f32[8,1,2912]{2,1,0:T(1,128)S(1)}, u32[]{:S(2)}, u32[]{:S(2)}) async-start(f32[8,1,2912]{2,1,0:T(1,128)} %reshape.398), calls=%async_computation | async-start | bytes 188416 | tf_op jit(solution)/shard_map/all_to_all | solution.py:27
  14.7 1.8 reshape.400
  16.5 5.5 %all-to-all-done = f32[8,1,2912]{2,1,0:T(1,128)S(1)} async-done(((f32[8,1,2912]{2,1,0:T(1,128)}), f32[8,1,2912]{2,1,0:T(1,128)S(1)}, u32[]{:S(2)}, u32[]{:S(2)}) %all-to-all-start) | async-done | bytes 93216 | tf_op jit(solution)/shard_map/all_to_all | solution.py:27
  22.0 7.5 %all-to-all-start.1 = ((f32[32,1,2912]{2,1,0:T(1,128)}), f32[32,1,2912]{2,1,0:T(1,128)S(1)}, u32[]{:S(2)}, u32[]{:S(2)}) async-start(f32[32,1,2912]{2,1,0:T(1,128)} %reshape.400), calls=%async_computation.1 | async-start | bytes 753664 | tf_op jit(solution)/shard_map/all_to_all | solution.py:27
  29.5 2.0 compare_select_fusion
  33.4 4.5 %all-to-all-done.1 = f32[32,1,2912]{2,1,0:T(1,128)S(1)} async-done(((f32[32,1,2912]{2,1,0:T(1,128)}), f32[32,1,2912]{2,1,0:T(1,128)S(1)}, u32[]{:S(2)}, u32[]{:S(2)}) %all-to-all-start.1) | async-done | bytes 372768 | tf_op jit(solution)/shard_map/all_to_all | solution.py:27
  40.6 45.0 %while.35 = (s32[]{:T(128)}, f32[3,16,1792]{2,1,0:T(8,128)S(1)}, f32[8,3,16,56]{3,0,2,1:T(8,128)S(1)}, f32[8,56,1792]{2,1,0:T(8,128)}, f32[8,4,56]{2,1,0:T(4,128...) while((s32[]{:T(128)}, f32[3,16,1792]{2,1,0:T(8,128)S(1)}, ...), condition=%wide.region_2.3_spmd.clone, body=%wide.region_0.2_spmd.clone.sunk | while | flops 236888064 | bytes 9123691 | solution.py:121
  42.4 2.1 fusion.132
  48.0 2.1 fusion.132
  50.1 1.7 fusion.133
  53.6 2.1 fusion.132
  59.3 2.1 fusion.132
  64.9 2.1 fusion.132
  66.9 1.7 fusion.133
  70.5 2.1 fusion.132
  76.1 2.1 fusion.132
  81.7 2.1 fusion.132
  83.8 1.7 fusion.133
  87.7 12.1 %all_to_all.40 = f32[32,1,2688]{2,1,0:T(1,128)S(1)} all-to-all(f32[32,1,2688]{2,1,0:T(1,128)S(1)} %reshape.402), channel_id=1, replica_groups=mesh['row'=32,'col'=8] {'row'}, dimensions={0} | all-to-all | bytes 688128 | tf_op jit(solution)/shard_map/all_to_all | solution.py:17
  102.8 6.8 %all-to-all-start.3 = ((f32[8,1,2688]{2,1,0:T(1,128)}), f32[8,1,2688]{2,1,0:T(1,128)S(1)}, u32[]{:S(2)}, u32[]{:S(2)}) async-start(f32[8,1,2688]{2,1,0:T(1,128)} %reshape.404), calls=%async_computation.3 | async-start | bytes 172032 | tf_op jit(solution)/shard_map/all_to_all | solution.py:40
  109.7 7.6 %all-to-all-done.3 = f32[8,1,2688]{2,1,0:T(1,128)S(1)} async-done(((f32[8,1,2688]{2,1,0:T(1,128)}), f32[8,1,2688]{2,1,0:T(1,128)S(1)}, u32[]{:S(2)}, u32[]{:S(2)}) %all-to-all-start.3) | async-done | bytes 86048 | tf_op jit(solution)/shard_map/all_to_all | solution.py:40
  118.2 44.6 %while.36 = (s32[]{:T(128)}, f32[3,16,1792]{2,1,0:T(8,128)S(1)}, f32[8,3,16,56]{3,2,1,0:T(8,128)S(1)}, f32[8,56,1792]{2,1,0:T(8,128)}, f32[8,4,56]{2,1,0:T(4,128...) while((s32[]{:T(128)}, f32[3,16,1792]{2,1,0:T(8,128)S(1)}, ...), condition=%wide.region_6.7_spmd.clone, body=%wide.region_4.6_spmd.clone.sunk | while | flops 236888064 | bytes 9131659 | solution.py:121
  120.0 2.1 fusion.138
  125.6 2.1 fusion.138
  131.2 2.1 fusion.138
  133.2 1.7 fusion.139
  136.8 2.1 fusion.138
  142.3 2.1 fusion.138
  147.9 2.1 fusion.138
  153.5 2.1 fusion.138
  159.1 2.1 fusion.138
  161.1 1.7 fusion.139
  165.0 12.3 %all_to_all.41 = f32[32,1,2688]{2,1,0:T(1,128)S(1)} all-to-all(f32[32,1,2688]{2,1,0:T(1,128)S(1)} %reshape.406), channel_id=1, replica_groups=mesh['row'=32,'col'=8] {'row'}, dimensions={0} | all-to-all | bytes 688128 | tf_op jit(solution)/shard_map/all_to_all | solution.py:17
  180.9 5.5 %all-to-all-start.5 = ((f32[8,1,2688]{2,1,0:T(1,128)}), f32[8,1,2688]{2,1,0:T(1,128)S(1)}, u32[]{:S(2)}, u32[]{:S(2)}) async-start(f32[8,1,2688]{2,1,0:T(1,128)} %reshape.408), calls=%async_computation.5 | async-start | bytes 172032 | tf_op jit(solution)/shard_map/all_to_all | solution.py:40
  186.4 7.5 %all-to-all-done.5 = f32[8,1,2688]{2,1,0:T(1,128)S(1)} async-done(((f32[8,1,2688]{2,1,0:T(1,128)}), f32[8,1,2688]{2,1,0:T(1,128)S(1)}, u32[]{:S(2)}, u32[]{:S(2)}) %all-to-all-start.5) | async-done | bytes 86048 | tf_op jit(solution)/shard_map/all_to_all | solution.py:40
  195.0 81.0 %while.37 = (s32[]{:T(128)}, f32[3,1792]{1,0:T(4,128)S(1)}, f32[8,3,56]{2,1,0:T(4,128)S(1)}, f32[8,56,1792]{2,1,0:T(8,128)}, f32[8,4,56]{2,1,0:T(4,128)S(1)}, /*...) while((s32[]{:T(128)}, f32[3,1792]{1,0:T(4,128)S(1)}, ...), condition=%wide.region_17.18_spmd.clone, body=%wide.region_8.17_spmd.clone.sunk | while | flops 248187520 | bytes 19899200 | solution.py:148
  196.8 3.7 %fusion.142 = (f32[3,56,1792]{2,1,0:T(8,128)S(1)}, f32[3,56,1792]{2,1,0:T(8,128)S(1)}) fusion(f32[3,56,1792]{2,1,0:T(8,128)S(1)} %get-tuple-element.447, f32[3,56,1792]{2,1,0:T(8,128)S(1)} %get-tuple-element.448, f32[3,16,1792]{2,1,0:T(8,128)S(1)} %get-tuple-element.532, f32[8,3,16,56]{3,2,1,0:T(8,128)S(1)} %get-tuple-element.531, ...), kind=kOutput, calls=%fused_computation.99.clone.1 | convolution fusion | flops 176418816 | bytes 5185540 | tf_op jit(solution)/shard_map/while/body/eval_jaxpr/transpose(jvp(abij,bpj->api))/dot_general | solution.py:71
  200.7 2.0 multiply_reduce_fusion.9
  202.7 1.7 fusion.144
  206.9 3.7 %fusion.142 = (f32[3,56,1792]{2,1,0:T(8,128)S(1)}, f32[3,56,1792]{2,1,0:T(8,128)S(1)}) fusion(f32[3,56,1792]{2,1,0:T(8,128)S(1)} %get-tuple-element.447, f32[3,56,1792]{2,1,0:T(8,128)S(1)} %get-tuple-element.448, f32[3,16,1792]{2,1,0:T(8,128)S(1)} %get-tuple-element.532, f32[8,3,16,56]{3,2,1,0:T(8,128)S(1)} %get-tuple-element.531, ...), kind=kOutput, calls=%fused_computation.99.clone.1 | convolution fusion | flops 176418816 | bytes 5185540 | tf_op jit(solution)/shard_map/while/body/eval_jaxpr/transpose(jvp(abij,bpj->api))/dot_general | solution.py:71
  210.8 2.0 multiply_reduce_fusion.9
  212.8 1.7 fusion.144
  217.0 3.7 %fusion.142 = (f32[3,56,1792]{2,1,0:T(8,128)S(1)}, f32[3,56,1792]{2,1,0:T(8,128)S(1)}) fusion(f32[3,56,1792]{2,1,0:T(8,128)S(1)} %get-tuple-element.447, f32[3,56,1792]{2,1,0:T(8,128)S(1)} %get-tuple-element.448, f32[3,16,1792]{2,1,0:T(8,128)S(1)} %get-tuple-element.532, f32[8,3,16,56]{3,2,1,0:T(8,128)S(1)} %get-tuple-element.531, ...), kind=kOutput, calls=%fused_computation.99.clone.1 | convolution fusion | flops 176418816 | bytes 5185540 | tf_op jit(solution)/shard_map/while/body/eval_jaxpr/transpose(jvp(abij,bpj->api))/dot_general | solution.py:71
  220.9 2.0 multiply_reduce_fusion.9
  222.9 1.7 fusion.144
  227.1 3.7 %fusion.142 = (f32[3,56,1792]{2,1,0:T(8,128)S(1)}, f32[3,56,1792]{2,1,0:T(8,128)S(1)}) fusion(f32[3,56,1792]{2,1,0:T(8,128)S(1)} %get-tuple-element.447, f32[3,56,1792]{2,1,0:T(8,128)S(1)} %get-tuple-element.448, f32[3,16,1792]{2,1,0:T(8,128)S(1)} %get-tuple-element.532, f32[8,3,16,56]{3,2,1,0:T(8,128)S(1)} %get-tuple-element.531, ...), kind=kOutput, calls=%fused_computation.99.clone.1 | convolution fusion | flops 176418816 | bytes 5185540 | tf_op jit(solution)/shard_map/while/body/eval_jaxpr/transpose(jvp(abij,bpj->api))/dot_general | solution.py:71
  231.1 2.0 multiply_reduce_fusion.9
  233.0 1.7 fusion.144
  237.2 3.7 %fusion.142 = (f32[3,56,1792]{2,1,0:T(8,128)S(1)}, f32[3,56,1792]{2,1,0:T(8,128)S(1)}) fusion(f32[3,56,1792]{2,1,0:T(8,128)S(1)} %get-tuple-element.447, f32[3,56,1792]{2,1,0:T(8,128)S(1)} %get-tuple-element.448, f32[3,16,1792]{2,1,0:T(8,128)S(1)} %get-tuple-element.532, f32[8,3,16,56]{3,2,1,0:T(8,128)S(1)} %get-tuple-element.531, ...), kind=kOutput, calls=%fused_computation.99.clone.1 | convolution fusion | flops 176418816 | bytes 5185540 | tf_op jit(solution)/shard_map/while/body/eval_jaxpr/transpose(jvp(abij,bpj->api))/dot_general | solution.py:71
  241.2 2.0 multiply_reduce_fusion.9
  243.1 1.7 fusion.144
  247.3 3.7 %fusion.142 = (f32[3,56,1792]{2,1,0:T(8,128)S(1)}, f32[3,56,1792]{2,1,0:T(8,128)S(1)}) fusion(f32[3,56,1792]{2,1,0:T(8,128)S(1)} %get-tuple-element.447, f32[3,56,1792]{2,1,0:T(8,128)S(1)} %get-tuple-element.448, f32[3,16,1792]{2,1,0:T(8,128)S(1)} %get-tuple-element.532, f32[8,3,16,56]{3,2,1,0:T(8,128)S(1)} %get-tuple-element.531, ...), kind=kOutput, calls=%fused_computation.99.clone.1 | convolution fusion | flops 176418816 | bytes 5185540 | tf_op jit(solution)/shard_map/while/body/eval_jaxpr/transpose(jvp(abij,bpj->api))/dot_general | solution.py:71
  251.3 2.0 multiply_reduce_fusion.9
  253.3 1.7 fusion.144
  257.5 3.7 %fusion.142 = (f32[3,56,1792]{2,1,0:T(8,128)S(1)}, f32[3,56,1792]{2,1,0:T(8,128)S(1)}) fusion(f32[3,56,1792]{2,1,0:T(8,128)S(1)} %get-tuple-element.447, f32[3,56,1792]{2,1,0:T(8,128)S(1)} %get-tuple-element.448, f32[3,16,1792]{2,1,0:T(8,128)S(1)} %get-tuple-element.532, f32[8,3,16,56]{3,2,1,0:T(8,128)S(1)} %get-tuple-element.531, ...), kind=kOutput, calls=%fused_computation.99.clone.1 | convolution fusion | flops 176418816 | bytes 5185540 | tf_op jit(solution)/shard_map/while/body/eval_jaxpr/transpose(jvp(abij,bpj->api))/dot_general | solution.py:71
  261.4 2.0 multiply_reduce_fusion.9
  263.4 1.7 fusion.144
  267.6 3.7 %fusion.142 = (f32[3,56,1792]{2,1,0:T(8,128)S(1)}, f32[3,56,1792]{2,1,0:T(8,128)S(1)}) fusion(f32[3,56,1792]{2,1,0:T(8,128)S(1)} %get-tuple-element.447, f32[3,56,1792]{2,1,0:T(8,128)S(1)} %get-tuple-element.448, f32[3,16,1792]{2,1,0:T(8,128)S(1)} %get-tuple-element.532, f32[8,3,16,56]{3,2,1,0:T(8,128)S(1)} %get-tuple-element.531, ...), kind=kOutput, calls=%fused_computation.99.clone.1 | convolution fusion | flops 176418816 | bytes 5185540 | tf_op jit(solution)/shard_map/while/body/eval_jaxpr/transpose(jvp(abij,bpj->api))/dot_general | solution.py:71
  271.5 2.0 multiply_reduce_fusion.9
  273.5 1.7 fusion.144
  276.6 4.3 %all-to-all-start.6 = ((f32[8,1,168]{2,1,0:T(1,128)}), f32[8,1,168]{2,1,0:T(1,128)S(1)}, u32[]{:S(2)}, u32[]{:S(2)}) async-start(f32[8,1,168]{2,1,0:T(1,128)} %reshape.410), calls=%async_computation.6 | async-start | bytes 16384 | tf_op jit(solution)/shard_map/all_to_all | solution.py:17
  281.8 6.2 %all-to-all-done.6 = f32[8,1,168]{2,1,0:T(1,128)S(1)} async-done(((f32[8,1,168]{2,1,0:T(1,128)}), f32[8,1,168]{2,1,0:T(1,128)S(1)}, u32[]{:S(2)}, u32[]{:S(2)}) %all-to-all-start.6) | async-done | bytes 5408 | tf_op jit(solution)/shard_map/all_to_all | solution.py:17
  288.0 3.9 %all-to-all-start.7 = ((f32[32,1,168]{2,1,0:T(1,128)}), f32[32,1,168]{2,1,0:T(1,128)S(1)}, u32[]{:S(2)}, u32[]{:S(2)}) async-start(f32[32,1,168]{2,1,0:T(1,128)} %reshape.412), calls=%async_computation.7 | async-start | bytes 65536 | tf_op jit(solution)/shard_map/all_to_all | solution.py:17
  292.6 6.4 %all-to-all-done.7 = f32[32,1,168]{2,1,0:T(1,128)S(1)} async-done(((f32[32,1,168]{2,1,0:T(1,128)}), f32[32,1,168]{2,1,0:T(1,128)S(1)}, u32[]{:S(2)}, u32[]{:S(2)}) %all-to-all-start.7) | async-done | bytes 21536 | tf_op jit(solution)/shard_map/all_to_all | solution.py:17
  (314 shorter events, 92.5 us)
Async XLA Ops:
  0.6 13.8 %copy-start.2 = (s32[8,32]{1,0:T(8,128)S(1)}, s32[8,32]{1,0:T(8,128)}, u32[]{:S(2)}) copy-start(s32[8,32]{1,0:T(8,128)} %param.15) | copy-start | bytes 3076
  4.4 17.6 %all-to-all-start = ((f32[8,1,2912]{2,1,0:T(1,128)}), f32[8,1,2912]{2,1,0:T(1,128)S(1)}, u32[]{:S(2)}, u32[]{:S(2)}) async-start(f32[8,1,2912]{2,1,0:T(1,128)} %reshape.398), calls=%async_computation | async-start | bytes 188416 | tf_op jit(solution)/shard_map/all_to_all | solution.py:27
  22.0 16.0 %all-to-all-start.1 = ((f32[32,1,2912]{2,1,0:T(1,128)}), f32[32,1,2912]{2,1,0:T(1,128)S(1)}, u32[]{:S(2)}, u32[]{:S(2)}) async-start(f32[32,1,2912]{2,1,0:T(1,128)} %reshape.400), calls=%async_computation.1 | async-start | bytes 753664 | tf_op jit(solution)/shard_map/all_to_all | solution.py:27
  99.8 2.1 copy-start
  99.8 2.2 copy-start.1
  102.8 14.4 %all-to-all-start.3 = ((f32[8,1,2688]{2,1,0:T(1,128)}), f32[8,1,2688]{2,1,0:T(1,128)S(1)}, u32[]{:S(2)}, u32[]{:S(2)}) async-start(f32[8,1,2688]{2,1,0:T(1,128)} %reshape.404), calls=%async_computation.3 | async-start | bytes 172032 | tf_op jit(solution)/shard_map/all_to_all | solution.py:40
  180.9 13.1 %all-to-all-start.5 = ((f32[8,1,2688]{2,1,0:T(1,128)}), f32[8,1,2688]{2,1,0:T(1,128)S(1)}, u32[]{:S(2)}, u32[]{:S(2)}) async-start(f32[8,1,2688]{2,1,0:T(1,128)} %reshape.408), calls=%async_computation.5 | async-start | bytes 172032 | tf_op jit(solution)/shard_map/all_to_all | solution.py:40
  276.6 11.4 %all-to-all-start.6 = ((f32[8,1,168]{2,1,0:T(1,128)}), f32[8,1,168]{2,1,0:T(1,128)S(1)}, u32[]{:S(2)}, u32[]{:S(2)}) async-start(f32[8,1,168]{2,1,0:T(1,128)} %reshape.410), calls=%async_computation.6 | async-start | bytes 16384 | tf_op jit(solution)/shard_map/all_to_all | solution.py:17
  288.0 11.0 %all-to-all-start.7 = ((f32[32,1,168]{2,1,0:T(1,128)}), f32[32,1,168]{2,1,0:T(1,128)S(1)}, u32[]{:S(2)}, u32[]{:S(2)}) async-start(f32[32,1,168]{2,1,0:T(1,128)} %reshape.412), calls=%async_computation.7 | async-start | bytes 65536 | tf_op jit(solution)/shard_map/all_to_all | solution.py:17
